TPU v7x, 512 devices: a whole 4x4x16 slice. The times are simulated.
512 devices in a mesh: seq: 64 (over y, z), tp: 8 (over x, core).
Axes of the slice: x: 4, y: 4, z: 16, core: 2. Of those that a mesh axis runs over, the one named last changes fastest.
Arguments:
- crop_features: bfloat16 [192, 21, 21, 1536], P('seq'), may hold values from -45 to 45
- crop_counts: int32 [64], replicated, may hold values from 1 to 3, as said below
- first_crop: int32 [64], replicated, may hold values from 0 to 127, as said below
- tile_embed: bfloat16 [3, 1536], replicated, may hold values from -3 to 3
- dw_weight: bfloat16 [49, 1536], replicated, may hold values from -0.875 to 0.875
- conv_bias: bfloat16 [1536], replicated, may hold values from -3 to 3
- ln_gain: bfloat16 [1536], replicated, may hold values from 0.099609375 to 1.8984375
- ln_bias: bfloat16 [1536], replicated, may hold values from -2 to 2
- w_up: bfloat16 [1536, 6144], P('seq', 'tp'), may hold values from -0.15625 to 0.15625
- b_up: bfloat16 [6144], P('tp'), may hold values from -3 to 3
- w_down: bfloat16 [6144, 1536], P('tp', 'seq'), may hold values from -0.078125 to 0.078125
- b_down: bfloat16 [1536], P('tp'), may hold values from -2 to 2
- gamma: float32 [1536], P('tp'), may hold values from 0.5 to 2
Outputs:
- visual_rows: bfloat16 [128, 21, 21, 1536], P('seq', None, None, 'tp')
Inputs may be any that keep to these rules, and one draw needn't show every extreme that they name: `crop_counts`: the counts sum to 128; 3 is reached in every draw. first_crop[0] is 0 and the entries never fall; device d holds first_crop[d+1] - first_crop[d] crops (the last device 128 - first_crop[last]), at most 3, and some device holds exactly 3; |first_crop[d] - d * 2| <= 1.
All inputs are finite; a program needn't handle non-finite values.
Results may differ from a plain program's by a relative error of at most 0.009.
Values may be sent and summed in bfloat16 or wider, within the bound.
No kernel may reach another device: no remote copies, remote signals or barrier semaphores. Data moves between devices by JAX's collectives and lax.ppermute only.
A program may use at most 128 MiB of HBM per device.

v0:
```python
import jax
import jax.numpy as jnp
from jax import lax
from jax.sharding import PartitionSpec as P

CROPS_DEV = 2


def from_behind(block, axis, distance):
    devices = range(lax.axis_size(axis))
    route = [(i - distance, i) for i in devices if i - distance in devices]
    return lax.ppermute(block, axis, route)


def regroup(slot_data, seq_index, first_held, held_limit, per_dev):

    def outgoing(offset_dev):
        target = (seq_index + offset_dev) * per_dev + jnp.arange(per_dev, dtype=jnp.int32)
        slot_idx = jnp.clip(target - first_held, 0, slot_data.shape[0] - 1)
        is_valid = (target >= first_held) & (target < held_limit)
        picked = jnp.take(slot_data, slot_idx, axis=0)
        return jnp.where(is_valid[:, None, None, None], picked, jnp.zeros_like(picked))

    result = outgoing(0)
    for offset_dev in (1, -1):
        result = result + from_behind(outgoing(offset_dev), "seq", offset_dev)
    return result


def encode(
    block_data,
    crop_ids,
    crop_counts,
    tile_embed,
    dw_weight,
    conv_bias,
    ln_gain,
    ln_bias,
    w_up,
    b_up,
    w_down,
    b_down,
    gamma,
):
    crop_number = block_data.shape[0]
    grid_size = block_data.shape[1]
    channels = block_data.shape[3]
    kernel_side = 7
    image_start = jnp.cumsum(crop_counts) - crop_counts
    image_begin = jnp.max(
        jnp.where(image_start[None, :] <= crop_ids[:, None], image_start[None, :], 0), axis=1
    )
    place_ids = crop_ids - image_begin
    choose = (
        place_ids[:, None] == jnp.arange(tile_embed.shape[0], dtype=jnp.int32)[None, :]
    ).astype(jnp.float32)
    tile_rows = jnp.sum(choose[:, :, None] * tile_embed.astype(jnp.float32)[None, :, :], axis=1)
    block_in = block_data.astype(jnp.float32) + tile_rows[:, None, None, :]
    padded = jnp.pad(block_in, ((0, 0), (3, 3), (3, 3), (0, 0)))
    conv_sum = jnp.zeros_like(block_in)
    for row_shift in range(kernel_side):
        for col_shift in range(kernel_side):
            conv_sum = conv_sum + padded[
                :, row_shift : row_shift + grid_size, col_shift : col_shift + grid_size, :
            ] * dw_weight[row_shift * kernel_side + col_shift].astype(jnp.float32)
    cell_rows = crop_number * grid_size * grid_size
    conv_out = (conv_sum + conv_bias.astype(jnp.float32)).reshape(cell_rows, channels)
    ln_mean = jnp.mean(conv_out, axis=1, keepdims=True)
    ln_var = jnp.mean((conv_out - ln_mean) ** 2, axis=1, keepdims=True)
    normed = (
        (conv_out - ln_mean) / jnp.sqrt(ln_var + 1e-06) * ln_gain.astype(jnp.float32)
        + ln_bias.astype(jnp.float32)
    ).astype(jnp.bfloat16)
    up_whole, down_whole = (
        lax.all_gather(w_up, "seq", axis=0, tiled=True),
        lax.all_gather(w_down, "seq", axis=1, tiled=True),
    )
    pre_act = jnp.dot(normed, up_whole, preferred_element_type=jnp.float32)
    hidden = jax.nn.gelu(pre_act + b_up.astype(jnp.float32), approximate=False).astype(jnp.bfloat16)
    partial_value = jnp.dot(hidden, down_whole, preferred_element_type=jnp.float32)
    summed = lax.psum_scatter(
        partial_value.astype(jnp.bfloat16), "tp", scatter_dimension=1, tiled=True
    ).astype(jnp.float32)
    out_width = b_down.shape[0]
    offset = lax.axis_index("tp") * out_width
    residual = lax.dynamic_slice_in_dim(block_in.reshape(cell_rows, channels), offset, out_width, 1)
    result = residual + gamma * (summed + b_down.astype(jnp.float32))
    return result.astype(jnp.bfloat16).reshape(crop_number, grid_size, grid_size, out_width)


def per_device(
    crop_features,
    crop_counts,
    first_crop,
    tile_embed,
    dw_weight,
    conv_bias,
    ln_gain,
    ln_bias,
    w_up,
    b_up,
    w_down,
    b_down,
    gamma,
):
    seq_count = lax.axis_size("seq")
    seq_index = lax.axis_index("seq")
    per_dev = CROPS_DEV
    slot_count = crop_features.shape[0]
    crop_total = per_dev * seq_count
    first_held = lax.dynamic_index_in_dim(first_crop, seq_index, 0, keepdims=False)
    next_first = lax.dynamic_index_in_dim(
        first_crop, jnp.minimum(seq_index + 1, seq_count - 1), 0, keepdims=False
    )
    held_limit = jnp.where(seq_index + 1 < seq_count, next_first, crop_total)
    held_ids = first_held + jnp.arange(slot_count, dtype=jnp.int32)
    encoded = encode(
        crop_features,
        held_ids,
        crop_counts,
        tile_embed,
        dw_weight,
        conv_bias,
        ln_gain,
        ln_bias,
        w_up,
        b_up,
        w_down,
        b_down,
        gamma,
    )
    visual_rows = regroup(encoded, seq_index, first_held, held_limit, per_dev)
    return visual_rows


def solution(mesh):
    placed = (
        P("seq", None, None, None),
        P(),
        P(),
        P(),
        P(),
        P(),
        P(),
        P(),
        P("seq", "tp"),
        P("tp"),
        P("tp", "seq"),
        P("tp"),
        P("tp"),
    )
    return jax.shard_map(
        per_device,
        mesh=mesh,
        in_specs=placed,
        out_specs=P("seq", None, None, "tp"),
        check_vma=False,
    )
```

profile of v0, /device:TPU:31, one launch (start us, length us, event | category | flops | bytes accessed | tf_op | source)
XLA Modules:
  0.0 392.1 jit_solution(10020580241406690454)
XLA Ops:
  6.5 0.7 all-gather.5.cloned.1.call-update
  7.3 0.7 all-gather.3.cloned.1.call-update
  8.0 0.0 reduce-scatter.2.cloned.1.call-start
  8.1 1.2 convert_reduce_fusion.46
  9.3 1.6 convert_reduce_fusion.48
  10.9 1.6 convert_reduce_fusion.47
  12.5 0.7 convert_element_type.537
  13.2 0.7 copy.20
  14.0 0.1 reduce-window.9
  14.1 0.1 reduce.2
  14.2 0.7 sub.39
  14.8 1.3 fusion.144
  16.2 0.5 iota_add_fusion.2
  16.7 0.2 select_reduce_fusion
  16.9 0.5 fusion.141
  17.5 0.1 fusion.110
  17.5 0.7 convert_element_type.636
  18.2 0.1 multiply_reduce_fusion.1
  18.3 7.2 %convert_add_fusion = f32[3,21,21,1536]{3,2,1,0:T(8,128)} fusion(bf16[3,21,21,1536]{3,2,1,0:T(8,128)(2,1)} %param.15, f32[3,1536]{1,0:T(4,128)S(1)} %multiply_reduce_fusion.1), kind=kLoop, calls=%fused_computation.149 | loop fusion | flops 4064256 | bytes 12211200 | tf_op jit(solution)/shard_map/add | solution.py:58
  25.5 179.8 %fusion.142 = (f32[3,21,21]{2,1,0:T(8,128)S(1)}, f32[3,21,21,1536]{3,2,1,0:T(8,128)}) fusion(f32[1536]{0:T(1024)S(1)} %convert_element_type.636, f32[1536]{0:T(1024)S(1)} %get-tuple-element.53, f32[1536]{0:T(1024)S(1)} %get-tuple-element.54, f32[1536]{0:T(1024)S(1)} %get-tuple-element.7, f32[1536]{0:T(1024)S(1)} %get-tuple-element.8, ...), kind=kLoop, calls=%fused_computation.281 | loop fusion | flops 201179344 | bytes 16569516 | tf_op jit(solution)/shard_map/reduce_sum | solution.py:68
  205.3 9.4 %reshape.478 = f32[1323,1536]{1,0:T(8,128)} reshape(f32[3,21,21,1536]{3,2,1,0:T(8,128)} %get-tuple-element.62) | data formatting | bytes 16257024 | tf_op jit(solution)/shard_map/reshape | solution.py:67
  214.8 0.1 div.17
  215.0 4.8 %multiply_reduce_fusion = f32[3,21,21]{2,1,0:T(8,128)S(1)} fusion(f32[3,21,21,1536]{3,2,1,0:T(8,128)} %get-tuple-element.62, f32[3,21,21]{2,1,0:T(8,128)S(1)} %broadcast_multiply_fusion), kind=kLoop, calls=%fused_computation.148 | loop fusion | flops 6095061 | bytes 8139096 | tf_op jit(solution)/shard_map/reduce_sum | solution.py:69
  219.8 0.1 sqrt.12
  220.0 66.0 %all-gather.3.cloned.1.call-done = bf16[1536,768]{1,0:T(8,128)(2,1)} async-done(((bf16[24,768]{1,0:T(8,128)(2,1)}), bf16[1536,768]{1,0:T(8,128)(2,1)}) %all-gather.3.cloned.1.call-update) | async-done | bytes 2359312 | tf_op jit(solution)/shard_map/all_gather | solution.py:75
  285.9 21.7 %convolution_convert_fusion = bf16[1323,1536]{0,1:T(8,128)(2,1)} fusion(bf16[768,1536]{0,1:T(8,128)(2,1)} %all-gather.5.cloned.1.call-done, bf16[1536,768]{1,0:T(8,128)(2,1)} %all-gather.3.cloned.1.call-done, f32[1323,1536]{1,0:T(8,128)} %reshape.478, f32[1536]{0:T(1024)S(1)} %convert_element_type.638, f32[1536]{0:T(1024)S(1)} %convert_element_type.637, ...), kind=kOutput, calls=%fused_computation.151 | convolution fusion | flops 6321950208 | bytes 16937304 | tf_op jit(solution)/shard_map/dot_general | solution.py:80
  307.7 9.4 %reshape.477 = f32[1323,1536]{1,0:T(8,128)} reshape(f32[3,21,21,1536]{3,2,1,0:T(8,128)} %convert_add_fusion) | data formatting | bytes 16257024 | tf_op jit(solution)/shard_map/reshape | solution.py:86
  317.0 1.7 constant_dynamic-slice_fusion
  318.8 0.4 copy.24
  319.9 0.6 compare_and_fusion.4
  320.4 0.6 compare_and_fusion.1
  321.0 0.6 compare_and_fusion
  321.6 36.5 %reduce-scatter.2.cloned.1.call-done = bf16[1323,192]{0,1:T(8,128)(2,1)} async-done(((bf16[1323,1536]{0,1:T(8,128)(2,1)}), bf16[1323,192]{0,1:T(8,128)(2,1)}) %reduce-scatter.2.cloned.1.call-update) | async-done | bytes 508048 | tf_op jit(solution)/shard_map/reduce_scatter | solution.py:81
  358.1 1.4 add_convert_fusion.6
  359.5 0.3 copy.22
  359.7 0.3 reshape.479
  360.1 0.6 gather_fusion.2
  360.7 0.1 select_select_fusion
  360.8 6.0 %collective-permute-start.1 = (bf16[2,21,21,192]{3,2,1,0:T(8,128)(2,1)S(1)}, bf16[2,21,21,192]{3,2,1,0:T(8,128)(2,1)S(1)}, u32[]{:S(2)}, u32[]{:S(2)}) collective-permute-start(bf16[2,21,21,192]{3,2,1,0:T(8,128)(2,1)S(1)} %select_select_fusion), channel_id=1, source_target_pairs={{8,0},{16,8},{24,16},{32,24},{40,32},{48,40},{56,48},{64,56},{72,6... | collective-permute-start | bytes 1016072 | tf_op jit(solution)/shard_map/ppermute | solution.py:12
  366.8 0.6 gather_fusion.1
  367.4 0.1 select_select_fusion.1
  367.5 1.9 collective-permute-start
  369.4 0.6 compare_and_fusion.2
  370.0 0.6 gather_fusion
  370.6 6.8 %collective-permute-done.1 = bf16[2,21,21,192]{3,2,1,0:T(8,128)(2,1)S(1)} collective-permute-done((bf16[2,21,21,192]{3,2,1,0:T(8,128)(2,1)S(1)}, bf16[2,21,21,192]{3,2,1,0:T(8,128)(2,1)S(1)}, u32[]{:S(2)}, u32[]{:S(2)}) %collective-permute-start.1) | collective-permute-done | bytes 338720 | tf_op jit(solution)/shard_map/ppermute | solution.py:12
  377.4 6.9 %collective-permute-done = bf16[2,21,21,192]{3,2,1,0:T(8,128)(2,1)S(1)} collective-permute-done((bf16[2,21,21,192]{3,2,1,0:T(8,128)(2,1)S(1)}, bf16[2,21,21,192]{3,2,1,0:T(8,128)(2,1)S(1)}, u32[]{:S(2)}, u32[]{:S(2)}) %collective-permute-start) | collective-permute-done | bytes 338720 | tf_op jit(solution)/shard_map/ppermute | solution.py:12
  384.3 0.2 fusion.109
  384.5 1.1 copy.23
  (23 shorter events, 0.2 us)
Async XLA Ops:
  6.5 213.4 %all-gather.5.cloned.1.call-start = ((), (), s32[]{:S(2)}) async-start(), calls=%async_computation.2 | async-start | bytes 2396160 | tf_op jit(solution)/shard_map/all_gather | solution.py:76
  7.3 278.7 %all-gather.3.cloned.1.call-start = ((), (), s32[]{:S(2)}) async-start(), calls=%async_computation.1 | async-start | bytes 2396160 | tf_op jit(solution)/shard_map/all_gather | solution.py:75
  8.0 350.1 %reduce-scatter.2.cloned.1.call-start = ((), (), s32[]{:S(2)}) async-start(), calls=%async_computation.3 | async-start | bytes 4866048 | tf_op jit(solution)/shard_map/reduce_scatter | solution.py:81
  205.3 9.5 %copy-start = (bf16[1536]{0:T(1024)(128)(2,1)S(1)}, bf16[1536]{0:T(1024)(128)(2,1)}, u32[]{:S(2)}) copy-start(bf16[1536]{0:T(1024)(128)(2,1)} %param.22) | copy-start | bytes 9220
  205.3 9.5 %copy-start.1 = (bf16[1536]{0:T(1024)(128)(2,1)S(1)}, bf16[1536]{0:T(1024)(128)(2,1)}, u32[]{:S(2)}) copy-start(bf16[1536]{0:T(1024)(128)(2,1)} %param.21) | copy-start | bytes 9220
  205.3 14.6 %copy-start.2 = (bf16[768]{0:T(1024)(128)(2,1)S(1)}, bf16[768]{0:T(1024)(128)(2,1)}, u32[]{:S(2)}) copy-start(bf16[768]{0:T(1024)(128)(2,1)} %param.24) | copy-start | bytes 4612
  307.6 11.6 %copy-start.4 = (bf16[192]{0:T(256)(128)(2,1)S(1)}, bf16[192]{0:T(256)(128)(2,1)}, u32[]{:S(2)}) copy-start(bf16[192]{0:T(256)(128)(2,1)} %param.26) | copy-start | bytes 1156
  307.6 50.4 %copy-start.3 = (f32[192]{0:T(256)S(1)}, f32[192]{0:T(256)}, u32[]{:S(2)}) copy-start(f32[192]{0:T(256)} %param.27) | copy-start | bytes 2308
  360.8 16.6 %collective-permute-start.1 = (bf16[2,21,21,192]{3,2,1,0:T(8,128)(2,1)S(1)}, bf16[2,21,21,192]{3,2,1,0:T(8,128)(2,1)S(1)}, u32[]{:S(2)}, u32[]{:S(2)}) collective-permute-start(bf16[2,21,21,192]{3,2,1,0:T(8,128)(2,1)S(1)} %select_select_fusion), channel_id=1, source_target_pairs={{8,0},{16,8},{24,16},{32,24},{40,32},{48,40},{56,48},{64,56},{72,6... | collective-permute-start | bytes 1016072 | tf_op jit(solution)/shard_map/ppermute | solution.py:12
  367.5 16.8 %collective-permute-start = (bf16[2,21,21,192]{3,2,1,0:T(8,128)(2,1)S(1)}, bf16[2,21,21,192]{3,2,1,0:T(8,128)(2,1)S(1)}, u32[]{:S(2)}, u32[]{:S(2)}) collective-permute-start(bf16[2,21,21,192]{3,2,1,0:T(8,128)(2,1)S(1)} %select_select_fusion.1), channel_id=1, source_target_pairs={{0,8},{8,16},{16,24},{24,32},{32,40},{40,48},{48,56},{56,64},{64,7... | collective-permute-start | bytes 1016072 | tf_op jit(solution)/shard_map/ppermute | solution.py:12
Sparse Core Ops, SparseCore 0:
  10.3 135.3 all-gather.4
  148.7 137.1 all-gather.2
  307.8 50.2 reduce-scatter.1
where the time goes:
time: 393 us; the launch traced here: 392 us
  other arithmetic  204 us (52%)
  waiting for transfers between devices  118 us (30%)
  local copies, waits for them, and re-layouts  26.8 us (7%)
  matrix products  21.7 us (6%)
  between operations  14.1 us (4%)
  starting transfers between devices  7.98 us (2%)
    reduce_sum x1, other arithmetic, encode(): ln_mean = jnp.mean(conv_out, axis=1, keepdims=True)  180 us
    all_gather x1, waiting for transfers between devices, encode(): lax.all_gather(w_up, 'seq', axis=0, tiled=True)  66 us
    reduce_scatter x1, waiting for transfers between devices, encode(): lax.psum_scatter(partial_value.astype(jnp.bfloat16), 'tp', scatter_dimens...  36.5 us
    dot_general x1, matrix products, encode(): jnp.dot(hidden, down_whole, preferred_element_type=jnp.float32)  21.7 us
    ppermute x2, waiting for transfers between devices, from_behind(): return lax.ppermute(block, axis, route)  13.7 us
    reshape x1, local copies, waits for them, and re-layouts, encode(): (conv_sum + conv_bias.astype(jnp.float32)).reshape(cell_rows, channels)  9.45 us
    reshape x1, local copies, waits for them, and re-layouts, encode(): block_in.reshape(cell_rows, channels)  9.35 us
    ppermute x2, starting transfers between devices, from_behind(): return lax.ppermute(block, axis, route)  7.9 us
  transfers between devices with their start and end apart: 5, of which 4 were waited for; matrix products, arithmetic and copies ran while one was open for 58% of the time, Pallas kernels for 0%

commit v1 on v0

--- a/solution.py
+++ b/solution.py
@@ -72,7 +72,10 @@
         + ln_bias.astype(jnp.float32)
     ).astype(jnp.bfloat16)
     up_whole, down_whole = (
-        lax.all_gather(w_up, "seq", axis=0, tiled=True),
+        jnp.concatenate(
+            lax.all_to_all(jnp.stack([w_up for _ in range(lax.axis_size("seq"))]), "seq", 0, 0),
+            axis=0,
+        ),
         lax.all_gather(w_down, "seq", axis=1, tiled=True),
     )
     pre_act = jnp.dot(normed, up_whole, preferred_element_type=jnp.float32)

time: 393 us -> 343 us (0.87)
  waiting for transfers between devices: 118 us -> 45.5 us
  starting transfers between devices: 7.98 us -> 26 us
  other arithmetic: 204 us -> 208 us
    all_gather x1 -> x0, waiting for transfers between devices: 66 us -> none  [encode(): lax.all_gather(w_up, 'seq', axis=0, tiled=True)]
    all_to_all x0 -> x1, starting transfers between devices: none -> 18.1 us  [encode(): lax.all_to_all(jnp.stack([w_up for _ in range(lax.axis_size('seq'))]), 's...]
    reshape x1 -> x0, local copies, waits for them, and re-layouts: 9.45 us -> none  [encode(): (conv_sum + conv_bias.astype(jnp.float32)).reshape(cell_rows, channels)]
    convert_element_type x0 -> x1, local copies, waits for them, and re-layouts: none -> 7.22 us  [encode(): normed = ((conv_out - ln_mean) / jnp.sqrt(ln_var + 1e-06) * ln_gain.astyp...]
    reduce_scatter x1, waiting for transfers between devices: 36.5 us -> 31.2 us  [encode(): lax.psum_scatter(partial_value.astype(jnp.bfloat16), 'tp', scatter_dimens...]
  transfers between devices with their start and end apart: 5 -> 5, of which waited for: 4 -> 3; matrix products, arithmetic and copies ran while one was open for 58% -> 68% of each run, Pallas kernels for 0% -> 0%
where the time goes in v1:
time: 343 us; the launch traced here: 341 us
  other arithmetic  208 us (61%)
  waiting for transfers between devices  45.5 us (13%)
  local copies, waits for them, and re-layouts  28.1 us (8%)
  starting transfers between devices  26 us (8%)
  matrix products  19.1 us (6%)
  between operations  14.3 us (4%)
    reduce_sum x1, other arithmetic, encode(): ln_mean = jnp.mean(conv_out, axis=1, keepdims=True)  179 us
    reduce_scatter x1, waiting for transfers between devices, encode(): lax.psum_scatter(partial_value.astype(jnp.bfloat16), 'tp', scatter_dimens...  31.2 us
    dot_general x1, matrix products, encode(): jnp.dot(hidden, down_whole, preferred_element_type=jnp.float32)  19.1 us
    all_to_all x1, starting transfers between devices, encode(): lax.all_to_all(jnp.stack([w_up for _ in range(lax.axis_size('seq'))]), 's...  18.1 us
    ppermute x2, waiting for transfers between devices, from_behind(): return lax.ppermute(block, axis, route)  13.5 us
    reshape x1, local copies, waits for them, and re-layouts, encode(): block_in.reshape(cell_rows, channels)  9.41 us
    ppermute x2, starting transfers between devices, from_behind(): return lax.ppermute(block, axis, route)  7.83 us
    convert_element_type x1, local copies, waits for them, and re-layouts, encode(): normed = ((conv_out - ln_mean) / jnp.sqrt(ln_var + 1e-06) * ln_gain.astyp...  7.22 us
  transfers between devices with their start and end apart: 5, of which 3 were waited for; matrix products, arithmetic and copies ran while one was open for 68% of the time, Pallas kernels for 0%

profile of v1, /device:TPU:31, one launch (start us, length us, event | category | flops | bytes accessed | tf_op | source)
XLA Modules:
  0.0 341.3 jit_solution(9310153967586162304)
XLA Ops:
  6.5 0.7 all-gather.2.cloned.1.call-update
  7.3 2.4 stack.2
  9.7 18.1 %all-to-all-start = ((bf16[64,24,768]{2,1,0:T(8,128)(2,1)}), bf16[64,24,768]{2,1,0:T(8,128)(2,1)S(1)}, u32[]{:S(2)}, u32[]{:S(2)}) async-start(bf16[64,24,768]{2,1,0:T(8,128)(2,1)} %stack.2), calls=%async_computation | async-start | bytes 4718592 | tf_op jit(solution)/shard_map/all_to_all | solution.py:76
  27.9 0.0 reduce-scatter.2.cloned.1.call-start
  27.9 1.2 convert_reduce_fusion.46
  29.1 1.7 convert_reduce_fusion.48
  30.8 1.6 convert_reduce_fusion.47
  32.4 0.7 convert_element_type.540
  33.1 0.7 copy.20
  33.9 0.1 reduce-window.9
  34.0 0.1 reduce.2
  34.1 0.7 sub.36
  34.7 1.4 fusion.143
  36.1 0.7 iota_add_fusion.2
  36.8 0.2 select_reduce_fusion
  37.0 0.7 fusion.140
  37.7 0.1 fusion.109
  37.8 0.7 convert_element_type.639
  38.5 0.1 multiply_reduce_fusion.1
  38.6 7.2 %convert_add_fusion = f32[3,21,21,1536]{3,2,1,0:T(8,128)} fusion(bf16[3,21,21,1536]{3,2,1,0:T(8,128)(2,1)} %param.15, f32[3,1536]{1,0:T(4,128)S(1)} %multiply_reduce_fusion.1), kind=kLoop, calls=%fused_computation.150 | loop fusion | flops 4064256 | bytes 12211200 | tf_op jit(solution)/shard_map/add | solution.py:58
  45.8 179.5 %fusion.141 = (f32[3,21,21]{2,1,0:T(8,128)S(1)}, f32[3,21,21,1536]{3,2,1,0:T(8,128)}) fusion(f32[1536]{0:T(1024)S(1)} %convert_element_type.639, f32[1536]{0:T(1024)S(1)} %get-tuple-element.53, f32[1536]{0:T(1024)S(1)} %get-tuple-element.54, f32[1536]{0:T(1024)S(1)} %get-tuple-element.7, f32[1536]{0:T(1024)S(1)} %get-tuple-element.8, ...), kind=kLoop, calls=%fused_computation.280 | loop fusion | flops 201179344 | bytes 16569516 | tf_op jit(solution)/shard_map/reduce_sum | solution.py:68
  225.4 4.9 %multiply_reduce_fusion = f32[3,21,21]{2,1,0:T(8,128)S(1)} fusion(f32[3,21,21,1536]{3,2,1,0:T(8,128)} %get-tuple-element.62, f32[3,21,21]{2,1,0:T(8,128)S(1)} %broadcast_multiply_fusion), kind=kLoop, calls=%fused_computation.149 | loop fusion | flops 6095061 | bytes 8139096 | tf_op jit(solution)/shard_map/reduce_sum | solution.py:69
  230.3 1.3 copy-done
  231.6 3.4 add_convert_fusion
  235.0 7.2 %convert_element_type.643 = bf16[1323,1536]{1,0:T(8,128)(2,1)} reshape(bf16[3,21,21,1536]{3,2,1,0:T(8,128)(2,1)} %add_convert_fusion) | data formatting | bytes 8128512 | tf_op jit(solution)/shard_map/convert_element_type | solution.py:73
  242.2 19.1 %convolution_convert_fusion = bf16[1323,1536]{0,1:T(8,128)(2,1)} fusion(bf16[768,1536]{0,1:T(8,128)(2,1)} %all-gather.2.cloned.1.call-done, bf16[1323,1536]{1,0:T(8,128)(2,1)} %convert_element_type.643, bf16[1536,768]{1,0:T(8,128)(2,1)S(1)} %bitcast.7, f32[768]{0:T(1024)S(1)} %convert_element_type.644), kind=kOutput, calls=%fused_computation.151 | convolution fusion | flops 6311789568 | bytes 12850176 | tf_op jit(solution)/shard_map/dot_general | solution.py:83
  261.4 9.4 %reshape.492 = f32[1323,1536]{1,0:T(8,128)} reshape(f32[3,21,21,1536]{3,2,1,0:T(8,128)} %convert_add_fusion) | data formatting | bytes 16257024 | tf_op jit(solution)/shard_map/reshape | solution.py:89
  270.8 1.7 constant_dynamic-slice_fusion
  272.5 0.4 copy.24
  273.6 0.7 compare_and_fusion.4
  274.3 0.7 compare_and_fusion.1
  275.0 0.7 compare_and_fusion
  275.8 31.2 %reduce-scatter.2.cloned.1.call-done = bf16[1323,192]{0,1:T(8,128)(2,1)} async-done(((bf16[1323,1536]{0,1:T(8,128)(2,1)}), bf16[1323,192]{0,1:T(8,128)(2,1)}) %reduce-scatter.2.cloned.1.call-update) | async-done | bytes 508048 | tf_op jit(solution)/shard_map/reduce_scatter | solution.py:84
  307.0 1.4 add_convert_fusion.1
  308.4 0.3 copy.22
  308.7 0.3 reshape.494
  309.0 0.6 gather_fusion.2
  309.6 0.1 select_select_fusion
  309.7 5.9 %collective-permute-start.1 = (bf16[2,21,21,192]{3,2,1,0:T(8,128)(2,1)S(1)}, bf16[2,21,21,192]{3,2,1,0:T(8,128)(2,1)S(1)}, u32[]{:S(2)}, u32[]{:S(2)}) collective-permute-start(bf16[2,21,21,192]{3,2,1,0:T(8,128)(2,1)S(1)} %select_select_fusion), channel_id=1, source_target_pairs={{8,0},{16,8},{24,16},{32,24},{40,32},{48,40},{56,48},{64,56},{72,6... | collective-permute-start | bytes 1016072 | tf_op jit(solution)/shard_map/ppermute | solution.py:12
  315.6 0.6 gather_fusion.1
  316.2 0.1 select_select_fusion.1
  316.4 1.9 collective-permute-start
  318.3 0.7 compare_and_fusion.2
  319.0 0.6 gather_fusion
  319.6 6.6 %collective-permute-done.1 = bf16[2,21,21,192]{3,2,1,0:T(8,128)(2,1)S(1)} collective-permute-done((bf16[2,21,21,192]{3,2,1,0:T(8,128)(2,1)S(1)}, bf16[2,21,21,192]{3,2,1,0:T(8,128)(2,1)S(1)}, u32[]{:S(2)}, u32[]{:S(2)}) %collective-permute-start.1) | collective-permute-done | bytes 338720 | tf_op jit(solution)/shard_map/ppermute | solution.py:12
  326.2 6.9 %collective-permute-done = bf16[2,21,21,192]{3,2,1,0:T(8,128)(2,1)S(1)} collective-permute-done((bf16[2,21,21,192]{3,2,1,0:T(8,128)(2,1)S(1)}, bf16[2,21,21,192]{3,2,1,0:T(8,128)(2,1)S(1)}, u32[]{:S(2)}, u32[]{:S(2)}) %collective-permute-start) | collective-permute-done | bytes 338720 | tf_op jit(solution)/shard_map/ppermute | solution.py:12
  333.1 0.2 fusion.108
  333.3 1.1 copy.23
  (24 shorter events, 0.1 us)
Async XLA Ops:
  6.5 235.7 %all-gather.2.cloned.1.call-start = ((), (), s32[]{:S(2)}) async-start(), calls=%async_computation.2 | async-start | bytes 2396160 | tf_op jit(solution)/shard_map/all_gather | solution.py:79
  9.7 232.5 %all-to-all-start = ((bf16[64,24,768]{2,1,0:T(8,128)(2,1)}), bf16[64,24,768]{2,1,0:T(8,128)(2,1)S(1)}, u32[]{:S(2)}, u32[]{:S(2)}) async-start(bf16[64,24,768]{2,1,0:T(8,128)(2,1)} %stack.2), calls=%async_computation | async-start | bytes 4718592 | tf_op jit(solution)/shard_map/all_to_all | solution.py:76
  27.9 279.1 %reduce-scatter.2.cloned.1.call-start = ((), (), s32[]{:S(2)}) async-start(), calls=%async_computation.3 | async-start | bytes 4866048 | tf_op jit(solution)/shard_map/reduce_scatter | solution.py:84
  45.8 179.5 %copy-start.1 = (bf16[1536]{0:T(1024)(128)(2,1)S(1)}, bf16[1536]{0:T(1024)(128)(2,1)}, u32[]{:S(2)}) copy-start(bf16[1536]{0:T(1024)(128)(2,1)} %param.22) | copy-start | bytes 9220
  45.8 179.5 %copy-start.2 = (bf16[1536]{0:T(1024)(128)(2,1)S(1)}, bf16[1536]{0:T(1024)(128)(2,1)}, u32[]{:S(2)}) copy-start(bf16[1536]{0:T(1024)(128)(2,1)} %param.21) | copy-start | bytes 9220
  225.3 6.3 %copy-start = (f32[3,21,21,1536]{3,2,1,0:T(8,128)S(1)}, f32[3,21,21,1536]{3,2,1,0:T(8,128)}, u32[]{:S(2)}) copy-start(f32[3,21,21,1536]{3,2,1,0:T(8,128)} %get-tuple-element.62) | copy-start | bytes 24385540
  231.6 10.6 %copy-start.3 = (bf16[768]{0:T(1024)(128)(2,1)S(1)}, bf16[768]{0:T(1024)(128)(2,1)}, u32[]{:S(2)}) copy-start(bf16[768]{0:T(1024)(128)(2,1)} %param.24) | copy-start | bytes 4612
  261.3 11.6 %copy-start.5 = (bf16[192]{0:T(256)(128)(2,1)S(1)}, bf16[192]{0:T(256)(128)(2,1)}, u32[]{:S(2)}) copy-start(bf16[192]{0:T(256)(128)(2,1)} %param.26) | copy-start | bytes 1156
  261.4 45.6 %copy-start.4 = (f32[192]{0:T(256)S(1)}, f32[192]{0:T(256)}, u32[]{:S(2)}) copy-start(f32[192]{0:T(256)} %param.27) | copy-start | bytes 2308
  309.7 16.5 %collective-permute-start.1 = (bf16[2,21,21,192]{3,2,1,0:T(8,128)(2,1)S(1)}, bf16[2,21,21,192]{3,2,1,0:T(8,128)(2,1)S(1)}, u32[]{:S(2)}, u32[]{:S(2)}) collective-permute-start(bf16[2,21,21,192]{3,2,1,0:T(8,128)(2,1)S(1)} %select_select_fusion), channel_id=1, source_target_pairs={{8,0},{16,8},{24,16},{32,24},{40,32},{48,40},{56,48},{64,56},{72,6... | collective-permute-start | bytes 1016072 | tf_op jit(solution)/shard_map/ppermute | solution.py:12
  316.4 16.8 %collective-permute-start = (bf16[2,21,21,192]{3,2,1,0:T(8,128)(2,1)S(1)}, bf16[2,21,21,192]{3,2,1,0:T(8,128)(2,1)S(1)}, u32[]{:S(2)}, u32[]{:S(2)}) collective-permute-start(bf16[2,21,21,192]{3,2,1,0:T(8,128)(2,1)S(1)} %select_select_fusion.1), channel_id=1, source_target_pairs={{0,8},{8,16},{16,24},{24,32},{32,40},{40,48},{48,56},{56,64},{64,7... | collective-permute-start | bytes 1016072 | tf_op jit(solution)/shard_map/ppermute | solution.py:12
Sparse Core Ops, SparseCore 0:
  10.3 164.9 all-gather.1
  261.5 45.4 reduce-scatter.1
